TPU v7x, 512 devices: a whole 4x8x8 slice. The times are simulated.
512 devices in a mesh: ctx: 64 (over z_lo, x, y), head: 8 (over z_hi, core).
Axes of the slice: x: 4, y: 8, z: 8 (z_hi: 4, z_lo: 2; z = z_hi * 2 + z_lo), core: 2. Of those that a mesh axis runs over, the one named last changes fastest.
Arguments:
- queries: bfloat16 [10240, 8192], P(('ctx', 'head')), may hold values from -18 to 18
- keys: bfloat16 [10240, 1024], P(('ctx', 'head')), may hold values from -4.5 to 4.5
- values: bfloat16 [10240, 1024], P(('ctx', 'head')), may hold values from -12 to 12
- block_order: int32 [128], replicated, may hold values from 0 to 127, each once
Outputs:
- attended: bfloat16 [10240, 8192], P(('ctx', 'head'))
Inputs may be any that keep to these rules, and one draw needn't show every extreme that they name: Storage block b holds sequence block block_order[b], its tokens in order; block_order is a permutation.
All inputs are finite; a program needn't handle non-finite values.
Results may differ from a plain program's by a relative error of at most 0.0049.
Values may be sent and summed in bfloat16 or wider, within the bound.
No kernel may reach another device: no remote copies, remote signals or barrier semaphores. Data moves between devices by JAX's collectives and lax.ppermute only.
A program may use at most 64 MiB of HBM per device.

v0:
```python
import math
import jax
import jax.numpy as jnp
import numpy as np
from jax import lax
from jax.sharding import PartitionSpec as P

QUERY_HEADS = 64
VALUE_KEY_HEADS = 8
HEAD_DIMENSION = 128


def token_positions(block_order, row_ids, block_rows):
    block_ids = row_ids // block_rows
    block_table = jnp.arange(block_order.shape[0], dtype=jnp.int32)
    chosen = jnp.sum(
        jnp.where(block_ids[:, None] == block_table[None, :], block_order[None, :], 0), axis=1
    )
    return chosen * block_rows + row_ids % block_rows


def attend(states, query_block, query_pos, key_rows, value_rows, key_pos, key_heads, score_scale):
    max_old, total_old, weighted_old = states
    query_count = query_block.shape[0]
    head_size = key_rows.shape[1] // key_heads
    heads_per_group = query_block.shape[1] // (key_heads * head_size)
    head_total = key_heads * heads_per_group
    query_split = query_block.reshape(query_count, key_heads, heads_per_group, head_size)
    key_split = key_rows.reshape(-1, key_heads, head_size)
    value_split = value_rows.reshape(-1, key_heads, head_size)
    scores = (
        jnp.einsum("qkgd,nkd->kgqn", query_split, key_split, preferred_element_type=jnp.float32)
        * score_scale
    )
    visible = key_pos[None, :] <= query_pos[:, None]
    scores = jnp.where(visible[None, None], scores, -jnp.inf)
    max_prev = max_old.reshape(key_heads, heads_per_group, query_count)
    max_new = jnp.maximum(max_prev, jnp.max(scores, axis=3))
    weights = jnp.exp(scores - max_new[..., None])
    rescale = jnp.exp(max_prev - max_new)
    total_new = total_old.reshape(key_heads, heads_per_group, query_count) * rescale + jnp.sum(
        weights, axis=3
    )
    mixed_values = jnp.einsum(
        "kgqn,nkd->qkgd",
        weights.astype(jnp.bfloat16),
        value_split,
        preferred_element_type=jnp.float32,
    )
    weighted_new = (
        weighted_old.reshape(query_count, key_heads, heads_per_group, head_size)
        * jnp.transpose(rescale, (2, 0, 1))[..., None]
        + mixed_values
    )
    return (
        max_new.reshape(head_total, query_count),
        total_new.reshape(head_total, query_count),
        weighted_new.reshape(query_count, head_total * head_size),
    )


def on_device(queries, keys, values, block_order):
    head_count = lax.axis_size("head")
    ctx_index = lax.axis_index("ctx")
    tokens_per_shard = queries.shape[0]
    query_heads = QUERY_HEADS // head_count
    heads_per_group = QUERY_HEADS // VALUE_KEY_HEADS
    local_kv = max(1, query_heads // heads_per_group)
    score_scale = HEAD_DIMENSION ** (-0.5)
    placement_index = np.array(
        [
            slot_number * query_heads // heads_per_group + offset
            for slot_number in range(head_count)
            for offset in range(local_kv)
        ],
        dtype=np.int32,
    )
    key_placements = keys.reshape(tokens_per_shard, VALUE_KEY_HEADS, HEAD_DIMENSION)[
        :, placement_index, :
    ].reshape(tokens_per_shard, head_count * local_kv * HEAD_DIMENSION)
    value_placements = values.reshape(tokens_per_shard, VALUE_KEY_HEADS, HEAD_DIMENSION)[
        :, placement_index, :
    ].reshape(tokens_per_shard, head_count * local_kv * HEAD_DIMENSION)
    tok_ctx = tokens_per_shard * head_count
    block_rows = tok_ctx // 2
    query_pos = token_positions(
        block_order, ctx_index * tok_ctx + jnp.arange(tok_ctx, dtype=jnp.int32), block_rows
    )

    def make_fold(query_all, key_heads, position_of):

        def tile(states, key_rows, value_rows, key_pos):
            updated = []
            for number in range(2):
                query_block = query_all[number * block_rows : (number + 1) * block_rows]
                block_pos = query_pos[number * block_rows : (number + 1) * block_rows]
                reach = jnp.min(key_pos) <= jnp.max(block_pos)
                updated.append(
                    lax.cond(
                        reach,
                        lambda carry_state: attend(
                            carry_state,
                            query_block,
                            block_pos,
                            key_rows,
                            value_rows,
                            key_pos,
                            key_heads,
                            score_scale,
                        ),
                        lambda carry_state: carry_state,
                        states[number],
                    )
                )
            return tuple(updated)

        def fold_step(states, key_piece, first_row):
            key_rows, value_rows = key_piece
            count = key_rows.shape[0]
            key_pos = position_of(jnp.arange(count, dtype=jnp.int32))
            piece_rows = tok_ctx * math.gcd(count // tok_ctx, 4)
            splits = count // piece_rows

            def scan_step(carry_states, parts):
                return (tile(carry_states, parts[0], parts[1], parts[2]), None)

            states, unused = lax.scan(
                scan_step,
                states,
                (
                    key_rows.reshape(splits, piece_rows, -1),
                    value_rows.reshape(splits, piece_rows, -1),
                    key_pos.reshape(splits, piece_rows),
                ),
            )
            return states

        return fold_step

    local_q, local_k, local_v = (
        lax.all_to_all(queries, "head", split_axis=1, concat_axis=0, tiled=True),
        lax.all_to_all(key_placements, "head", split_axis=1, concat_axis=0, tiled=True),
        lax.all_to_all(value_placements, "head", split_axis=1, concat_axis=0, tiled=True),
    )

    def full_positions(row_ids):
        return token_positions(block_order, row_ids, block_rows)

    fold_each = make_fold(local_q, local_kv, full_positions)
    one_state = (
        jnp.full((query_heads, block_rows), -1e30, jnp.float32),
        jnp.zeros((query_heads, block_rows), jnp.float32),
        jnp.zeros((block_rows, query_heads * HEAD_DIMENSION), jnp.float32),
    )
    states = fold_each(
        (one_state, one_state),
        (
            lax.all_gather(local_k, "ctx", axis=0, tiled=True),
            lax.all_gather(local_v, "ctx", axis=0, tiled=True),
        ),
        jnp.int32(0),
    )
    total_all = jnp.concatenate([states[0][1], states[1][1]], axis=1)
    weighted_all = jnp.concatenate([states[0][2], states[1][2]], axis=0)
    weighted_all = weighted_all.reshape(tok_ctx, query_heads, HEAD_DIMENSION)
    attended = (
        (weighted_all / total_all.T[:, :, None])
        .reshape(tok_ctx, query_heads * HEAD_DIMENSION)
        .astype(jnp.bfloat16)
    )
    return lax.all_to_all(attended, "head", split_axis=0, concat_axis=1, tiled=True)


def solution(mesh):
    placed = (P(("ctx", "head"), None), P(("ctx", "head"), None), P(("ctx", "head"), None), P())
    return jax.shard_map(
        on_device, mesh=mesh, in_specs=placed, out_specs=P(("ctx", "head"), None), check_vma=False
    )
```

profile of v0, /device:TPU:62, one launch (start us, length us, event | category | flops | bytes accessed | tf_op | source)
XLA Modules:
  0.0 792.8 jit_solution(8596616769344484240)
XLA Ops:
  8.0 18.4 %all_to_all.67 = bf16[20,8,128]{2,0,1:T(8,128)(2,1)S(1)} all-to-all(bf16[20,8,128]{2,0,1:T(8,128)(2,1)S(1)} %bitcast.142), channel_id=1, replica_groups=mesh['ctx'=64,'head'=8] {'head'}, dimensions={1} | all-to-all | bytes 81920 | tf_op jit(solution)/shard_map/all_to_all | solution.py:142
  28.4 10.5 %all_to_all.68 = bf16[20,8,128]{2,0,1:T(8,128)(2,1)S(1)} all-to-all(bf16[20,8,128]{2,0,1:T(8,128)(2,1)S(1)} %bitcast.141), channel_id=1, replica_groups=mesh['ctx'=64,'head'=8] {'head'}, dimensions={1} | all-to-all | bytes 81920 | tf_op jit(solution)/shard_map/all_to_all | solution.py:143
  41.8 3.5 all-to-all-start.2
  45.3 6.3 select_reduce_fusion
  52.7 7.9 all-to-all-done.2
  60.7 264.9 %all-gather.3.cloned.1.call-done = bf16[10240,128]{1,0:T(8,128)(2,1)} async-done(((bf16[160,128]{1,0:T(8,128)(2,1)}), bf16[10240,128]{1,0:T(8,128)(2,1)}) %all-gather.3.cloned.1.call-update) | async-done | bytes 2621456 | tf_op jit(solution)/shard_map/all_gather | solution.py:158
  325.5 302.4 %all-gather.5.cloned.1.call-done = bf16[10240,128]{1,0:T(8,128)(2,1)} async-done(((bf16[160,128]{1,0:T(8,128)(2,1)}), bf16[10240,128]{1,0:T(8,128)(2,1)}) %all-gather.5.cloned.1.call-update) | async-done | bytes 2621456 | tf_op jit(solution)/shard_map/all_gather | solution.py:159
  628.0 135.3 %while.21 = (s32[]{:T(128)}, f32[8,80]{1,0:T(8,128)S(1)}, f32[8,80]{1,0:T(8,128)S(1)}, f32[80,1024]{1,0:T(8,128)S(1)}, f32[8,80]{1,0:T(8,128)S(1)}, /*index=5*/f...) while((s32[]{:T(128)}, f32[8,80]{1,0:T(8,128)S(1)}, ...), condition=%wide.region_14.15_spmd, body=%wide.region_4.14_spmd.sunk | while | flops 425599360 | bytes 17010988 | solution.py:127
  634.3 2.1 conditional.5
  642.8 2.1 conditional.5
  651.2 2.1 conditional.5
  659.7 2.1 conditional.5
  668.1 2.1 conditional.5
  676.6 2.1 conditional.5
  685.0 2.1 conditional.5
  693.5 2.1 conditional.5
  701.9 2.1 conditional.5
  710.4 2.1 conditional.5
  718.9 2.1 conditional.5
  727.3 2.1 conditional.5
  735.8 2.1 conditional.5
  744.2 2.1 conditional.5
  752.7 2.1 conditional.5
  764.1 20.6 %all_to_all.69 = bf16[8,20,1024]{2,1,0:T(8,128)(2,1)S(1)} all-to-all(bf16[8,20,1024]{2,1,0:T(8,128)(2,1)S(1)} %divide_convert_fusion), channel_id=1, replica_groups=mesh['ctx'=64,'head'=8] {'head'}, dimensions={0} | all-to-all | bytes 655360 | tf_op jit(solution)/shard_map/all_to_all | solution.py:171
  (447 shorter events, 135.6 us)
Async XLA Ops:
  6.5 319.0 %all-gather.3.cloned.1.call-start = ((), (), s32[]{:S(2)}) async-start(), calls=%async_computation.4 | async-start | bytes 2662400 | tf_op jit(solution)/shard_map/all_gather | solution.py:158
  27.0 600.9 %all-gather.5.cloned.1.call-start = ((), (), s32[]{:S(2)}) async-start(), calls=%async_computation.5 | async-start | bytes 2662400 | tf_op jit(solution)/shard_map/all_gather | solution.py:159
  28.4 16.9 %copy-start = (s32[128]{0:T(128)S(1)}, s32[128]{0:T(128)}, u32[]{:S(2)}) copy-start(s32[128]{0:T(128)} %param.16) | copy-start | bytes 1540
  41.8 18.8 %all-to-all-start.2 = ((bf16[20,8,1024]{2,0,1:T(8,128)(2,1)}), bf16[20,8,1024]{2,0,1:T(8,128)(2,1)S(1)}, u32[]{:S(2)}, u32[]{:S(2)}) async-start(bf16[20,8,1024]{2,0,1:T(8,128)(2,1)} %copy.40), calls=%async_computation.2 | async-start | bytes 786432 | tf_op jit(solution)/shard_map/all_to_all | solution.py:141
Sparse Core Ops, SparseCore 0:
  27.1 298.3 all-gather.2
  327.6 300.2 all-gather.4
where the time goes:
time: 794 us; the launch traced here: 793 us
  waiting for transfers between devices  575 us (72%)
  blocking collectives  49.5 us (6%)
  loops' own time  44.3 us (6%)
  other arithmetic  40.1 us (5%)
  matrix products  33.5 us (4%)
  local copies, waits for them, and re-layouts  33.1 us (4%)
  between operations  13.6 us (2%)
    all_gather x1, waiting for transfers between devices, on_device(): lax.all_gather(local_v, 'ctx', axis=0, tiled=True)  302 us
    all_gather x1, waiting for transfers between devices, on_device(): lax.all_gather(local_k, 'ctx', axis=0, tiled=True)  265 us
    another operation x1, loops' own time, fold_step(): lax.scan(scan_step, states, (key_rows.reshape(splits, piece_rows, -1), va...  41.5 us
    all_to_all x1, blocking collectives, on_device(): lax.all_to_all(attended, 'head', split_axis=0, concat_axis=1, tiled=True)  20.6 us
    reduce_sum x32, other arithmetic, attend(): jnp.sum(weights, axis=3)  18.5 us
    all_to_all x1, blocking collectives, on_device(): lax.all_to_all(key_placements, 'head', split_axis=1, concat_axis=0, tiled...  18.4 us
    dot_general x32, matrix products, attend(): jnp.einsum('qkgd,nkd->kgqn', query_split, key_split, preferred_element_ty...  17.7 us
    squeeze x16, local copies, waits for them, and re-layouts, fold_step(): lax.scan(scan_step, states, (key_rows.reshape(splits, piece_rows, -1), va...  16.4 us
  transfers between devices with their start and end apart: 3, of which 3 were waited for; matrix products, arithmetic and copies ran while one was open for 1% of the time, Pallas kernels for 0%

commit v1 on v0

--- a/solution.py
+++ b/solution.py
@@ -8,6 +8,11 @@
 QUERY_HEADS = 64
 VALUE_KEY_HEADS = 8
 HEAD_DIMENSION = 128
+
+
+def swapped_in(array, name, d):
+    repeated = jnp.stack([array] * lax.axis_size(name))
+    return jnp.concatenate(lax.all_to_all(repeated, name, 0, 0), axis=d)
 
 
 def token_positions(block_order, row_ids, block_rows):
@@ -154,10 +159,7 @@
     )
     states = fold_each(
         (one_state, one_state),
-        (
-            lax.all_gather(local_k, "ctx", axis=0, tiled=True),
-            lax.all_gather(local_v, "ctx", axis=0, tiled=True),
-        ),
+        (swapped_in(local_k, "ctx", 0), lax.all_gather(local_v, "ctx", axis=0, tiled=True)),
         jnp.int32(0),
     )
     total_all = jnp.concatenate([states[0][1], states[1][1]], axis=1)

time: 794 us -> 523 us (0.66)
  the two profiles are of different devices: /device:TPU:62 before, /device:TPU:1 now
where the time goes in v1:
time: 523 us; the launch traced here: 521 us
  waiting for transfers between devices  263 us (50%)
  blocking collectives  61.5 us (12%)
  loops' own time  45.4 us (9%)
  other arithmetic  39.1 us (7%)
  local copies, waits for them, and re-layouts  35.1 us (7%)
  starting transfers between devices  32.2 us (6%)
  matrix products  31.2 us (6%)
  between operations  13.6 us (3%)
    all_gather x1, waiting for transfers between devices, on_device(): lax.all_gather(local_v, 'ctx', axis=0, tiled=True)  241 us
    all_to_all x1, blocking collectives, on_device(): lax.all_to_all(attended, 'head', split_axis=0, concat_axis=1, tiled=True)  61.5 us
    another operation x1, loops' own time, fold_step(): lax.scan(scan_step, states, (key_rows.reshape(splits, piece_rows, -1), va...  42.7 us
    reduce_sum x30, other arithmetic, attend(): jnp.sum(weights, axis=3)  16.7 us
    dot_general x30, matrix products, attend(): jnp.einsum('qkgd,nkd->kgqn', query_split, key_split, preferred_element_ty...  16.6 us
    squeeze x16, local copies, waits for them, and re-layouts, fold_step(): lax.scan(scan_step, states, (key_rows.reshape(splits, piece_rows, -1), va...  16.4 us
    dot_general x30, matrix products, attend(): jnp.einsum('kgqn,nkd->qkgd', weights.astype(jnp.bfloat16), value_split, p...  14.6 us
    all_to_all x1, starting transfers between devices, swapped_in(): return jnp.concatenate(lax.all_to_all(repeated, name, 0, 0), axis=d)  12.3 us
  transfers between devices with their start and end apart: 5, of which 4 were waited for; matrix products, arithmetic and copies ran while one was open for 3% of the time, Pallas kernels for 0%

profile of v1, /device:TPU:1, one launch (start us, length us, event | category | flops | bytes accessed | tf_op | source)
XLA Modules:
  0.0 521.2 jit_solution(10992448271618052768)
XLA Ops:
  8.6 11.8 %all-to-all-start = ((bf16[20,8,128]{2,0,1:T(8,128)(2,1)}), bf16[20,8,128]{2,0,1:T(8,128)(2,1)S(1)}, u32[]{:S(2)}, u32[]{:S(2)}) async-start(bf16[20,8,128]{2,0,1:T(8,128)(2,1)} %bitcast.24), calls=%async_computation | async-start | bytes 98304 | tf_op jit(solution)/shard_map/all_to_all | solution.py:147
  22.4 5.5 %all-to-all-done = bf16[20,8,128]{2,0,1:T(8,128)(2,1)S(1)} async-done(((bf16[20,8,128]{2,0,1:T(8,128)(2,1)}), bf16[20,8,128]{2,0,1:T(8,128)(2,1)S(1)}, u32[]{:S(2)}, u32[]{:S(2)}) %all-to-all-start) | async-done | bytes 40992 | tf_op jit(solution)/shard_map/all_to_all | solution.py:147
  27.9 4.0 all-to-all-start.2
  34.1 5.2 all-to-all-done.2
  39.3 4.1 all-to-all-start.3
  44.1 11.2 %all-to-all-done.3 = bf16[20,8,1024]{2,0,1:T(8,128)(2,1)S(1)} async-done(((bf16[20,8,1024]{2,0,1:T(8,128)(2,1)}), bf16[20,8,1024]{2,0,1:T(8,128)(2,1)S(1)}, u32[]{:S(2)}, u32[]{:S(2)}) %all-to-all-start.3) | async-done | bytes 327712 | tf_op jit(solution)/shard_map/all_to_all | solution.py:146
  57.1 12.3 %all-to-all-start.1 = ((bf16[64,160,128]{2,1,0:T(8,128)(2,1)}), bf16[64,160,128]{2,1,0:T(8,128)(2,1)}, u32[]{:S(2)}, u32[]{:S(2)}) async-start(bf16[64,160,128]{2,1,0:T(8,128)(2,1)} %stack.5), calls=%async_computation.1 | async-start | bytes 5242880 | tf_op jit(solution)/shard_map/all_to_all | solution.py:15
  69.5 6.3 %select_reduce_fusion = s32[10240]{0:T(1024)S(1)} fusion(s32[128]{0:T(128)S(1)} %copy-done, s32[10240]{0:T(1024)S(1)} %add_select_fusion.1), kind=kLoop, calls=%fused_computation.44 | loop fusion | flops 3921920 | bytes 82432 | tf_op jit(solution)/shard_map/reduce_sum | solution.py:21
  76.9 241.1 %all-gather.2.cloned.1.call-done = bf16[10240,128]{1,0:T(8,128)(2,1)} async-done(((bf16[160,128]{1,0:T(8,128)(2,1)}), bf16[10240,128]{1,0:T(8,128)(2,1)}) %all-gather.2.cloned.1.call-update) | async-done | bytes 2621456 | tf_op jit(solution)/shard_map/all_gather | solution.py:162
  318.1 132.7 %while.21 = (s32[]{:T(128)}, f32[8,80]{1,0:T(8,128)S(1)}, f32[8,80]{1,0:T(8,128)S(1)}, f32[80,1024]{1,0:T(8,128)S(1)}, f32[8,80]{1,0:T(8,128)S(1)}, /*index=5*/f...) while((s32[]{:T(128)}, f32[8,80]{1,0:T(8,128)S(1)}, ...), condition=%wide.region_14.15_spmd, body=%wide.region_4.14_spmd.sunk | while | flops 425599360 | bytes 17010988 | solution.py:132
  333.1 2.1 conditional.5
  341.6 2.1 conditional.5
  350.2 2.1 conditional.5
  373.8 2.1 conditional.5
  380.3 2.1 conditional.5
  388.9 2.1 conditional.5
  397.4 2.1 conditional.5
  406.0 2.1 conditional.5
  414.5 2.1 conditional.5
  423.1 2.1 conditional.5
  431.6 2.1 conditional.5
  440.2 2.1 conditional.5
  448.7 2.1 conditional.5
  451.6 61.5 %all_to_all.69 = bf16[8,20,1024]{2,1,0:T(8,128)(2,1)S(1)} all-to-all(bf16[8,20,1024]{2,1,0:T(8,128)(2,1)S(1)} %divide_convert_fusion), channel_id=1, replica_groups=mesh['ctx'=64,'head'=8] {'head'}, dimensions={0} | all-to-all | bytes 655360 | tf_op jit(solution)/shard_map/all_to_all | solution.py:173
  (427 shorter events, 134.0 us)
Async XLA Ops:
  8.6 19.3 %all-to-all-start = ((bf16[20,8,128]{2,0,1:T(8,128)(2,1)}), bf16[20,8,128]{2,0,1:T(8,128)(2,1)S(1)}, u32[]{:S(2)}, u32[]{:S(2)}) async-start(bf16[20,8,128]{2,0,1:T(8,128)(2,1)} %bitcast.24), calls=%async_computation | async-start | bytes 98304 | tf_op jit(solution)/shard_map/all_to_all | solution.py:147
  27.9 11.4 %all-to-all-start.2 = ((bf16[20,8,128]{2,0,1:T(8,128)(2,1)}), bf16[20,8,128]{2,0,1:T(8,128)(2,1)S(1)}, u32[]{:S(2)}, u32[]{:S(2)}) async-start(bf16[20,8,128]{2,0,1:T(8,128)(2,1)} %bitcast.27), calls=%async_computation.2 | async-start | bytes 98304 | tf_op jit(solution)/shard_map/all_to_all | solution.py:148
  39.3 16.0 %all-to-all-start.3 = ((bf16[20,8,1024]{2,0,1:T(8,128)(2,1)}), bf16[20,8,1024]{2,0,1:T(8,128)(2,1)S(1)}, u32[]{:S(2)}, u32[]{:S(2)}) async-start(bf16[20,8,1024]{2,0,1:T(8,128)(2,1)} %copy.39), calls=%async_computation.3 | async-start | bytes 786432 | tf_op jit(solution)/shard_map/all_to_all | solution.py:146
  43.4 274.6 %all-gather.2.cloned.1.call-start = ((), (), s32[]{:S(2)}) async-start(), calls=%async_computation.5 | async-start | bytes 2662400 | tf_op jit(solution)/shard_map/all_gather | solution.py:162
  57.1 12.3 %copy-start = (s32[128]{0:T(128)S(1)}, s32[128]{0:T(128)}, u32[]{:S(2)}) copy-start(s32[128]{0:T(128)} %param.16) | copy-start | bytes 1540
  57.1 260.9 %all-to-all-start.1 = ((bf16[64,160,128]{2,1,0:T(8,128)(2,1)}), bf16[64,160,128]{2,1,0:T(8,128)(2,1)}, u32[]{:S(2)}, u32[]{:S(2)}) async-start(bf16[64,160,128]{2,1,0:T(8,128)(2,1)} %stack.5), calls=%async_computation.1 | async-start | bytes 5242880 | tf_op jit(solution)/shard_map/all_to_all | solution.py:15
Sparse Core Ops, SparseCore 0:
  46.3 271.7 all-gather.1
